TPU v7x, 256 devices: a whole 4x4x8 slice. The times are simulated.
256 devices in a mesh: fac: 4 (over y_lo, core), col: 64 (over y_hi, x, z).
Axes of the slice: x: 4, y: 4 (y_hi: 2, y_lo: 2; y = y_hi * 2 + y_lo), z: 8, core: 2. Of those that a mesh axis runs over, the one named last changes fastest.
Arguments:
- lower_factor: bfloat16 [1, 4, 4, 256, 256], P(None, 'fac', None, None, 'col'), may hold values from -0.1875 to 0.1875
- panel_inverse: float32 [1, 4, 256, 256], P(None, 'fac', None, 'col'), may hold values from -0.375 to 0.375
- right_side: float32 [1, 4, 256, 8192], P(None, 'fac', None, 'col'), may hold values from -0.1875 to 0.1875
- fill: int32 [4, 4], replicated, may hold values 0 or 1
Outputs:
- schur: float32 [8192, 4, 2048], P('col', 'fac')
All inputs are finite; a program needn't handle non-finite values.
Results may differ from a plain program's by a relative error of at most 0.0034.
Values may be sent and summed in bfloat16 or wider, within the bound.
No kernel may reach another device: no remote copies, remote signals or barrier semaphores. Data moves between devices by JAX's collectives and lax.ppermute only.
A program may use at most 64 MiB of HBM per device.

v0:
```python
import jax
import jax.numpy as jnp
from jax import lax
from jax.sharding import PartitionSpec as P


def broadcast(array, axis, root):
    mine = lax.axis_index(axis) == root
    return lax.psum(jnp.where(mine, array, jnp.zeros_like(array)), axis)


def per_device(lower_factor, panel_inverse, right_side, fill):
    panels = lower_factor.shape[0]
    fac_count = lax.axis_size("fac")
    my_index = lax.axis_index("fac")
    inverses = lax.all_gather(panel_inverse, "col", axis=3, tiled=True)[:, 0]
    pending = right_side[:, 0]
    solved = jnp.zeros(pending.shape, jnp.bfloat16)
    total_panels = panels * fac_count
    selector = (jnp.arange(fac_count) == my_index).astype(jnp.int32)
    for owner in range(fac_count):
        own_solve = jnp.dot(
            inverses[0],
            pending[0],
            precision=lax.Precision.HIGHEST,
            preferred_element_type=jnp.float32,
        ).astype(jnp.bfloat16)
        panel_rows = broadcast(own_solve, "fac", owner)
        solved = solved.at[0].set(jnp.where(my_index == owner, panel_rows, solved[0]))
        if owner + 1 < total_panels:
            later_blocks = lower_factor[0:, 0, owner]
            column_flags = fill[:, owner].reshape(panels, fac_count)
            flags = jnp.sum(column_flags * selector[None, :], axis=1)
            targets = jnp.arange(0, panels) * fac_count + my_index
            keep_mask = ((flags == 1) & (targets > owner)).astype(jnp.float32)
            update = jnp.einsum(
                "nab,bm->nam",
                lax.all_gather(later_blocks, "col", axis=2, tiled=True),
                panel_rows,
                preferred_element_type=jnp.float32,
            )
            pending = pending.at[0:].add(-keep_mask[:, None, None] * update)
    slab_flat = solved.reshape(-1, solved.shape[2])
    columns_dev = slab_flat.shape[1]
    share = columns_dev // fac_count
    all_rows = lax.all_gather(slab_flat, "fac", axis=0, tiled=True)
    my_share = lax.dynamic_slice_in_dim(all_rows, my_index * share, share, 1)
    products = lax.dot_general(
        all_rows,
        lax.all_gather(my_share, "col", axis=1, tiled=True),
        (((0,), (0,)), ((), ())),
        preferred_element_type=jnp.float32,
    )
    result = products[:, None, :]
    return result


def solution(mesh):
    return jax.shard_map(
        per_device,
        mesh=mesh,
        in_specs=(
            P(None, "fac", None, None, "col"),
            P(None, "fac", None, "col"),
            P(None, "fac", None, "col"),
            P(),
        ),
        out_specs=P("col", "fac", None),
        check_vma=False,
    )
```

profile of v0, /device:TPU:2, one launch (start us, length us, event | category | flops | bytes accessed | tf_op | source)
XLA Modules:
  0.0 919.4 jit_solution(4776379949293501510)
XLA Ops:
  6.5 0.0 all-reduce.5.cloned.1.call-start
  6.5 0.7 copy.21
  7.2 164.2 %all_gather.18 = f32[1,1,256,256]{2,1,0,3:T(1,128)S(1)} all-gather(f32[1,1,256,4]{2,1,0,3:T(1,128)S(1)} %copy.21), channel_id=1, replica_groups=mesh['fac'=4,'col'=64] {'col'}, dimensions={3}, use_global_device_ids=true | all-gather | bytes 266240 | tf_op jit(solution)/shard_map/all_gather | solution.py:16
  171.4 2.1 fusion.6
  173.6 0.0 all-reduce.5.cloned.1.call-update
  173.6 0.0 all-reduce.7.cloned.1.call-start
  173.6 1.0 slice_reduce_fusion
  174.6 0.7 fusion.28
  175.4 0.7 fusion.27
  176.0 1.0 copy.20
  177.7 175.3 %all-gather = bf16[1,1,1,256,256]{3,2,1,0,4:T(2,128)(2,1)S(1)} all-gather(bf16[1,1,1,256,4]{3,2,1,0,4:T(2,128)(2,1)S(1)} %copy.37), channel_id=2, replica_groups=mesh['fac'=4,'col'=64] {'col'}, dimensions={4}, use_global_device_ids=true | all-gather | bytes 133120 | tf_op jit(solution)/shard_map/all_gather | solution.py:38
  353.0 0.1 copy.23
  353.1 0.0 all-reduce.5.cloned.1.call-done
  353.2 0.0 copy-start
  353.2 1.1 fusion.3
  354.3 1.2 fusion.8
  355.5 0.0 all-reduce.7.cloned.1.call-update
  355.5 0.0 all-reduce.9.cloned.1.call-start
  355.6 0.6 fusion.26
  356.8 177.2 %all-gather.1 = bf16[1,1,1,256,256]{3,2,1,0,4:T(2,128)(2,1)S(1)} all-gather(bf16[1,1,1,256,4]{3,2,1,0,4:T(2,128)(2,1)S(1)} %copy.38), channel_id=3, replica_groups=mesh['fac'=4,'col'=64] {'col'}, dimensions={4}, use_global_device_ids=true | all-gather | bytes 133120 | tf_op jit(solution)/shard_map/all_gather | solution.py:38
  534.0 0.1 copy.26
  534.2 0.0 all-reduce.7.cloned.1.call-done
  534.2 1.0 fusion.4
  535.2 1.2 fusion.10
  536.5 0.0 all-reduce.9.cloned.1.call-update
  536.5 0.0 all-reduce.11.cloned.1.call-start
  536.5 0.7 fusion.25
  537.9 175.4 %all-gather.2 = bf16[1,1,1,256,256]{3,2,1,0,4:T(2,128)(2,1)S(1)} all-gather(bf16[1,1,1,256,4]{3,2,1,0,4:T(2,128)(2,1)S(1)} %copy.39), channel_id=4, replica_groups=mesh['fac'=4,'col'=64] {'col'}, dimensions={4}, use_global_device_ids=true | all-gather | bytes 133120 | tf_op jit(solution)/shard_map/all_gather | solution.py:38
  713.3 0.1 copy.29
  713.4 0.0 all-reduce.9.cloned.1.call-done
  713.4 1.0 fusion.5
  714.5 1.2 fusion.12
  715.7 0.0 all-reduce.11.cloned.1.call-update
  715.7 0.0 all-gather.5.cloned.1.call-start
  715.8 55.5 %all-reduce.11.cloned.1.call-done = bf16[256,128]{1,0:T(8,128)(2,1)} async-done(((bf16[256,128]{1,0:T(8,128)(2,1)}), bf16[256,128]{1,0:T(8,128)(2,1)}) %all-reduce.11.cloned.1.call-update) | async-done | bytes 65552 | tf_op jit(solution)/shard_map/psum | solution.py:9
  771.3 0.0 copy-done
  771.3 6.2 all_gather.22
  777.5 0.1 constant_dynamic-slice_fusion
  777.7 0.8 copy.31
  778.4 0.0 all-gather.5.cloned.1.call-update
  778.5 128.6 %all-gather.5.cloned.1.call-done = bf16[1024,2048]{0,1:T(8,128)(2,1)} async-done(((bf16[1024,32]{0,1:T(8,128)(2,1)}), bf16[1024,2048]{0,1:T(8,128)(2,1)}) %all-gather.5.cloned.1.call-update) | async-done | bytes 4194320 | tf_op jit(solution)/shard_map/all_gather | solution.py:50
  907.1 3.7 convolution_bitcast_fusion
  910.8 2.0 copy.32
  (4 shorter events, 0.0 us)
Async XLA Ops:
  6.5 346.6 %all-reduce.5.cloned.1.call-start = ((), (), s32[]{:S(2)}) async-start(), calls=%async_computation | async-start | bytes 131072 | tf_op jit(solution)/shard_map/psum | solution.py:9
  173.6 360.6 %all-reduce.7.cloned.1.call-start = ((), (), s32[]{:S(2)}) async-start(), calls=%async_computation.1 | async-start | bytes 131072 | tf_op jit(solution)/shard_map/psum | solution.py:9
  353.2 418.1 %copy-start = (bf16[256,128]{1,0:T(8,128)(2,1)S(1)}, bf16[256,128]{1,0:T(8,128)(2,1)}, u32[]{:S(2)}) copy-start(bf16[256,128]{1,0:T(8,128)(2,1)} %all-reduce.5.cloned.1.call-done) | copy-start | bytes 196612
  355.5 357.9 %all-reduce.9.cloned.1.call-start = ((), (), s32[]{:S(2)}) async-start(), calls=%async_computation.2 | async-start | bytes 131072 | tf_op jit(solution)/shard_map/psum | solution.py:9
  536.5 234.8 %all-reduce.11.cloned.1.call-start = ((), (), s32[]{:S(2)}) async-start(), calls=%async_computation.3 | async-start | bytes 131072 | tf_op jit(solution)/shard_map/psum | solution.py:9
  715.7 191.3 %all-gather.5.cloned.1.call-start = ((), (), s32[]{:S(2)}) async-start(), calls=%async_computation.4 | async-start | bytes 4259840 | tf_op jit(solution)/shard_map/all_gather | solution.py:50
Sparse Core Ops, SparseCore 0:
  173.7 54.0 all-reduce.4
  355.7 55.3 all-reduce.6
  536.6 54.0 all-reduce.8
  715.9 55.3 all-reduce.10
  778.6 128.4 all-gather.4
where the time goes:
time: 920 us; the launch traced here: 919 us
  blocking collectives  698 us (76%)
  waiting for transfers between devices  184 us (20%)
  between operations  15.1 us (2%)
  matrix products  12.7 us (1%)
    all_gather x3, blocking collectives, per_device(): lax.all_gather(later_blocks, 'col', axis=2, tiled=True)  528 us
    all_gather x1, blocking collectives, per_device(): inverses = lax.all_gather(panel_inverse, 'col', axis=3, tiled=True)[:, 0]  164 us
    all_gather x1, waiting for transfers between devices, per_device(): lax.all_gather(my_share, 'col', axis=1, tiled=True)  129 us
    psum x4, waiting for transfers between devices, broadcast(): return lax.psum(jnp.where(mine, array, jnp.zeros_like(array)), axis)  55.5 us
  transfers between devices with their start and end apart: 5, of which 2 were waited for; matrix products, arithmetic and copies ran while one was open for 1% of the time, Pallas kernels for 0%

commit v1 on v0

--- a/solution.py
+++ b/solution.py
@@ -2,6 +2,19 @@
 import jax.numpy as jnp
 from jax import lax
 from jax.sharding import PartitionSpec as P
+from jax.lax import all_to_all, psum
+
+
+def see_seats_all(local_x):
+    return jnp.concatenate(
+        all_to_all(
+            jnp.stack([local_x] * psum(1, axis_name="col")),
+            split_axis=0,
+            concat_axis=0,
+            axis_name="col",
+        ),
+        axis=2,
+    )
 
 
 def broadcast(array, axis, root):
@@ -35,7 +48,7 @@
             keep_mask = ((flags == 1) & (targets > owner)).astype(jnp.float32)
             update = jnp.einsum(
                 "nab,bm->nam",
-                lax.all_gather(later_blocks, "col", axis=2, tiled=True),
+                see_seats_all(later_blocks),
                 panel_rows,
                 preferred_element_type=jnp.float32,
             )

time: 920 us -> 523 us (0.57)
  blocking collectives: 698 us -> 167 us
  waiting for transfers between devices: 184 us -> 262 us
  starting transfers between devices: 0.17 us -> 53.9 us
    all_gather x3 -> x0, blocking collectives: 528 us -> none  [per_device(): lax.all_gather(later_blocks, 'col', axis=2, tiled=True)]
    psum x4, waiting for transfers between devices: 55.5 us -> 133 us  [broadcast(): return lax.psum(jnp.where(mine, array, jnp.zeros_like(array)), axis)]
    all_to_all x0 -> x3, starting transfers between devices: none -> 53.7 us  [see_seats_all(): all_to_all(jnp.stack([local_x] * psum(1, axis_name='col')), split_axis=0,...]
  transfers between devices with their start and end apart: 5 -> 8, of which waited for: 2 -> 5; matrix products, arithmetic and copies ran while one was open for 1% -> 2% of each run, Pallas kernels for 0% -> 0%
where the time goes in v1:
time: 523 us; the launch traced here: 522 us
  waiting for transfers between devices  262 us (50%)
  blocking collectives  167 us (32%)
  starting transfers between devices  53.9 us (10%)
  between operations  15.1 us (3%)
  matrix products  12.6 us (2%)
  local copies, waits for them, and re-layouts  8.54 us (2%)
    all_gather x1, blocking collectives, per_device(): inverses = lax.all_gather(panel_inverse, 'col', axis=3, tiled=True)[:, 0]  161 us
    psum x4, waiting for transfers between devices, broadcast(): return lax.psum(jnp.where(mine, array, jnp.zeros_like(array)), axis)  133 us
    all_gather x1, waiting for transfers between devices, per_device(): lax.all_gather(my_share, 'col', axis=1, tiled=True)  129 us
    all_to_all x3, starting transfers between devices, see_seats_all(): all_to_all(jnp.stack([local_x] * psum(1, axis_name='col')), split_axis=0,...  53.7 us
  transfers between devices with their start and end apart: 8, of which 5 were waited for; matrix products, arithmetic and copies ran while one was open for 2% of the time, Pallas kernels for 0%

profile of v1, /device:TPU:2, one launch (start us, length us, event | category | flops | bytes accessed | tf_op | source)
XLA Modules:
  0.0 522.1 jit_solution(3908540455276330916)
XLA Ops:
  6.5 0.7 slice_bitcast_fusion
  7.3 0.7 stack.9
  7.9 14.6 %all-to-all-start = ((bf16[64,1,256,4]{2,3,1,0:T(4,128)(2,1)}), bf16[64,1,256,4]{2,3,1,0:T(4,128)(2,1)S(1)}, u32[]{:S(2)}, u32[]{:S(2)}) async-start(bf16[64,1,256,4]{2,3,1,0:T(4,128)(2,1)} %stack.9), calls=%async_computation | async-start | bytes 262144 | tf_op jit(solution)/shard_map/all_to_all | solution.py:10
  22.6 0.0 all-reduce.5.cloned.1.call-start
  22.7 0.7 copy.19
  23.4 161.1 %all_gather.9 = f32[1,1,256,256]{2,1,0,3:T(1,128)S(1)} all-gather(f32[1,1,256,4]{2,1,0,3:T(1,128)S(1)} %copy.19), channel_id=1, replica_groups=mesh['fac'=4,'col'=64] {'col'}, dimensions={3}, use_global_device_ids=true | all-gather | bytes 266240 | tf_op jit(solution)/shard_map/all_gather | solution.py:29
  184.4 2.1 fusion.6
  186.5 0.0 all-reduce.5.cloned.1.call-update
  186.6 1.0 copy.18
  187.6 1.0 slice_reduce_fusion
  188.6 0.6 fusion.24
  189.8 0.0 all-to-all-done
  189.8 0.7 stack.10
  190.5 26.4 %all-to-all-start.1 = ((bf16[64,1,256,4]{2,3,1,0:T(4,128)(2,1)}), bf16[64,1,256,4]{2,3,1,0:T(4,128)(2,1)S(1)}, u32[]{:S(2)}, u32[]{:S(2)}) async-start(bf16[64,1,256,4]{2,3,1,0:T(4,128)(2,1)} %stack.10), calls=%async_computation.1 | async-start | bytes 262144 | tf_op jit(solution)/shard_map/all_to_all | solution.py:10
  216.9 0.0 all-reduce.7.cloned.1.call-start
  217.0 23.5 %all-reduce.5.cloned.1.call-done = bf16[256,128]{1,0:T(8,128)(2,1)} async-done(((bf16[256,128]{1,0:T(8,128)(2,1)}), bf16[256,128]{1,0:T(8,128)(2,1)}) %all-reduce.5.cloned.1.call-update) | async-done | bytes 65552 | tf_op jit(solution)/shard_map/psum | solution.py:22
  240.4 1.0 fusion.3
  241.5 1.2 fusion.8
  242.7 0.0 all-reduce.7.cloned.1.call-update
  242.7 0.7 fusion.23
  244.0 0.0 all-to-all-done.1
  244.1 0.7 stack.11
  244.7 12.7 %all-to-all-start.2 = ((bf16[64,1,256,4]{2,3,1,0:T(4,128)(2,1)}), bf16[64,1,256,4]{2,3,1,0:T(4,128)(2,1)S(1)}, u32[]{:S(2)}, u32[]{:S(2)}) async-start(bf16[64,1,256,4]{2,3,1,0:T(4,128)(2,1)} %stack.11), calls=%async_computation.2 | async-start | bytes 262144 | tf_op jit(solution)/shard_map/all_to_all | solution.py:10
  257.4 0.0 all-reduce.9.cloned.1.call-start
  257.5 27.6 %all-reduce.7.cloned.1.call-done = bf16[256,128]{1,0:T(8,128)(2,1)} async-done(((bf16[256,128]{1,0:T(8,128)(2,1)}), bf16[256,128]{1,0:T(8,128)(2,1)}) %all-reduce.7.cloned.1.call-update) | async-done | bytes 65552 | tf_op jit(solution)/shard_map/psum | solution.py:22
  285.1 1.0 fusion.4
  286.1 1.2 fusion.10
  287.4 0.0 all-reduce.9.cloned.1.call-update
  287.4 0.0 all-reduce.11.cloned.1.call-start
  287.4 0.7 fusion.22
  288.8 0.0 all-to-all-done.2
  288.8 40.6 %all-reduce.9.cloned.1.call-done = bf16[256,128]{1,0:T(8,128)(2,1)} async-done(((bf16[256,128]{1,0:T(8,128)(2,1)}), bf16[256,128]{1,0:T(8,128)(2,1)}) %all-reduce.9.cloned.1.call-update) | async-done | bytes 65552 | tf_op jit(solution)/shard_map/psum | solution.py:22
  329.4 1.0 fusion.5
  330.4 1.2 fusion.12
  331.6 0.0 all-reduce.11.cloned.1.call-update
  331.7 0.0 all-gather.2.cloned.1.call-start
  331.7 41.8 %all-reduce.11.cloned.1.call-done = bf16[256,128]{1,0:T(8,128)(2,1)} async-done(((bf16[256,128]{1,0:T(8,128)(2,1)}), bf16[256,128]{1,0:T(8,128)(2,1)}) %all-reduce.11.cloned.1.call-update) | async-done | bytes 65552 | tf_op jit(solution)/shard_map/psum | solution.py:22
  373.5 0.9 select_select_fusion
  374.3 5.9 %all_gather.10 = bf16[1024,128]{1,0:T(8,128)(2,1)S(1)} all-gather(bf16[256,128]{1,0:T(8,128)(2,1)S(1)} %select_select_fusion), channel_id=1, replica_groups=mesh['fac'=4,'col'=64] {'fac'}, dimensions={0}, use_global_device_ids=true | all-gather | bytes 327680 | tf_op jit(solution)/shard_map/all_gather | solution.py:59
  380.2 0.1 constant_dynamic-slice_fusion
  380.4 0.8 copy.23
  381.1 0.0 all-gather.2.cloned.1.call-update
  381.1 128.6 %all-gather.2.cloned.1.call-done = bf16[1024,2048]{0,1:T(8,128)(2,1)} async-done(((bf16[1024,32]{0,1:T(8,128)(2,1)}), bf16[1024,2048]{0,1:T(8,128)(2,1)}) %all-gather.2.cloned.1.call-update) | async-done | bytes 4194320 | tf_op jit(solution)/shard_map/all_gather | solution.py:63
  509.8 3.7 convolution_bitcast_fusion
  513.5 2.0 copy.24
  (3 shorter events, 0.1 us)
Async XLA Ops:
  7.9 181.9 %all-to-all-start = ((bf16[64,1,256,4]{2,3,1,0:T(4,128)(2,1)}), bf16[64,1,256,4]{2,3,1,0:T(4,128)(2,1)S(1)}, u32[]{:S(2)}, u32[]{:S(2)}) async-start(bf16[64,1,256,4]{2,3,1,0:T(4,128)(2,1)} %stack.9), calls=%async_computation | async-start | bytes 262144 | tf_op jit(solution)/shard_map/all_to_all | solution.py:10
  22.6 217.8 %all-reduce.5.cloned.1.call-start = ((), (), s32[]{:S(2)}) async-start(), calls=%async_computation.3 | async-start | bytes 131072 | tf_op jit(solution)/shard_map/psum | solution.py:22
  190.5 53.5 %all-to-all-start.1 = ((bf16[64,1,256,4]{2,3,1,0:T(4,128)(2,1)}), bf16[64,1,256,4]{2,3,1,0:T(4,128)(2,1)S(1)}, u32[]{:S(2)}, u32[]{:S(2)}) async-start(bf16[64,1,256,4]{2,3,1,0:T(4,128)(2,1)} %stack.10), calls=%async_computation.1 | async-start | bytes 262144 | tf_op jit(solution)/shard_map/all_to_all | solution.py:10
  216.9 68.2 %all-reduce.7.cloned.1.call-start = ((), (), s32[]{:S(2)}) async-start(), calls=%async_computation.4 | async-start | bytes 131072 | tf_op jit(solution)/shard_map/psum | solution.py:22
  244.7 44.0 %all-to-all-start.2 = ((bf16[64,1,256,4]{2,3,1,0:T(4,128)(2,1)}), bf16[64,1,256,4]{2,3,1,0:T(4,128)(2,1)S(1)}, u32[]{:S(2)}, u32[]{:S(2)}) async-start(bf16[64,1,256,4]{2,3,1,0:T(4,128)(2,1)} %stack.11), calls=%async_computation.2 | async-start | bytes 262144 | tf_op jit(solution)/shard_map/all_to_all | solution.py:10
  257.4 71.9 %all-reduce.9.cloned.1.call-start = ((), (), s32[]{:S(2)}) async-start(), calls=%async_computation.5 | async-start | bytes 131072 | tf_op jit(solution)/shard_map/psum | solution.py:22
  287.4 86.1 %all-reduce.11.cloned.1.call-start = ((), (), s32[]{:S(2)}) async-start(), calls=%async_computation.6 | async-start | bytes 131072 | tf_op jit(solution)/shard_map/psum | solution.py:22
  331.7 178.1 %all-gather.2.cloned.1.call-start = ((), (), s32[]{:S(2)}) async-start(), calls=%async_computation.7 | async-start | bytes 4259840 | tf_op jit(solution)/shard_map/all_gather | solution.py:63
Sparse Core Ops, SparseCore 0:
  186.7 53.7 all-reduce.4
  243.0 42.0 all-reduce.6
  287.7 41.5 all-reduce.8
  331.8 41.5 all-reduce.10
  381.3 128.4 all-gather.1
